TPU v7x, 32 devices: a whole 2x2x4 slice. The times are simulated.
32 devices in a mesh: dp: 16 (over z, y, core), seq: 2 (over x).
Axes of the slice: x: 2, y: 2, z: 4, core: 2. Of those that a mesh axis runs over, the one named last changes fastest.
Arguments:
- pre_act: bfloat16 [16, 512, 768], P('dp', 'seq'), may hold values from -6 to 6
- trunk_grad: bfloat16 [16, 256, 768], P('dp', None, 'seq'), may hold values from -6 to 6
- conv_weight: bfloat16 [5, 768, 768], P(None, 'dp'), may hold values from -0.09375 to 0.09375
- pair_weight: bfloat16 [768, 768], replicated, may hold values from -0.21875 to 0.21875
- donor_slots: int32 [16, 2, 2, 128], P('dp', 'seq'), may hold values from 0 to 255
- accept_slots: int32 [16, 2, 2, 128], P('dp', 'seq'), may hold values from 0 to 255
- junction_grad: float32 [16, 2, 2, 128], P('dp', 'seq'), may hold values from -6 to 6
- pair_counts: int32 [16, 2, 2], P('dp'), may hold values from 0 to 128, as said below
Outputs:
- input_grad: bfloat16 [16, 512, 768], P('dp', 'seq')
- pair_grad: float32 [768, 768], replicated
Inputs may be any that keep to these rules, and one draw needn't show every extreme that they name: pair_counts is at most 128; in every sample some acceptor slab has 128 live slots from every donor slab.
All inputs are finite; a program needn't handle non-finite values.
Results may differ from a plain program's by a relative error of at most 0.0061.
Values may be sent and summed in bfloat16 or wider, within the bound.
A program may use at most 64 MiB of HBM per device.

v0:
```python
import math
import jax
import jax.numpy as jnp
from jax import lax
from jax.sharding import PartitionSpec as P


def with_halo(x, sides, width):
    for axis, dim in sides:
        size, length = (lax.axis_size(axis), x.shape[dim])
        up = [(i, (i + 1) % size) for i in range(size - 1)]
        down = [(j, i) for i, j in up]
        last = lax.slice_in_dim(x, length - width, length, axis=dim)
        first = lax.slice_in_dim(x, 0, width, axis=dim)
        before = lax.ppermute(last, axis, up)
        after = lax.ppermute(first, axis, down)
        x = jnp.concatenate([before, x, after], axis=dim)
    return x


def gelu_parts(values):
    normal_cdf = 0.5 * (1.0 + jax.scipy.special.erf(values / math.sqrt(2.0)))
    density = jnp.exp(-0.5 * values * values) / math.sqrt(2.0 * math.pi)
    return (values * normal_cdf, normal_cdf + values * density)


def per_device(
    pre_act,
    trunk_grad,
    conv_weight,
    pair_weight,
    donor_slots,
    accept_slots,
    junction_grad,
    pair_counts,
):
    seq_count = lax.axis_size("seq")
    my_slab = lax.axis_index("seq")
    slab_len = pre_act.shape[1]
    channels = pre_act.shape[2]
    slot_count = donor_slots.shape[3]
    kernel = conv_weight.shape[0]
    half = kernel // 2
    act_f, slope = gelu_parts(pre_act[0].astype(jnp.float32))
    act = act_f.astype(jnp.bfloat16)
    arrived = lax.all_to_all(trunk_grad, "seq", split_axis=1, concat_axis=2, tiled=True)
    pooled = jnp.repeat(arrived[0].astype(jnp.float32) * 0.5, 2, axis=0)
    send_index = donor_slots[0, 0].reshape(-1)
    outgoing = act[send_index].reshape(seq_count, slot_count, channels)
    incoming = lax.all_to_all(outgoing, "seq", split_axis=0, concat_axis=0, tiled=True)
    donor_rows = incoming.reshape(-1, channels)
    accept_index = accept_slots[0, 0].reshape(-1)
    counts_in = lax.dynamic_index_in_dim(pair_counts[0], my_slab, axis=1, keepdims=False)
    live = jnp.arange(slot_count, dtype=jnp.int32)[None, :] < counts_in[:, None]
    slot_w = jnp.where(live, junction_grad[0, 0], 0.0).reshape(-1)
    accept_rows = act[accept_index]
    weighted = (slot_w[:, None] * accept_rows.astype(jnp.float32)).astype(jnp.bfloat16)
    accept_term = (
        jnp.dot(donor_rows, pair_weight, preferred_element_type=jnp.float32) * slot_w[:, None]
    )
    donor_term = lax.dot_general(
        weighted, pair_weight, (((1,), (1,)), ((), ())), preferred_element_type=jnp.float32
    ).astype(jnp.bfloat16)
    pair_part = lax.dot_general(
        donor_rows, weighted, (((0,), (0,)), ((), ())), preferred_element_type=jnp.float32
    )
    returned = lax.all_to_all(
        donor_term.reshape(seq_count, slot_count, channels),
        "seq",
        split_axis=0,
        concat_axis=0,
        tiled=True,
    )
    act_grad = (
        pooled.at[accept_index]
        .add(accept_term)
        .at[send_index]
        .add(returned.reshape(-1, channels).astype(jnp.float32))
    )
    conv_grad = (act_grad * slope).astype(jnp.bfloat16)
    padded = with_halo(conv_grad[None], (("seq", 1),), half)[0]
    piece = lax.all_gather(conv_weight, "dp", axis=1, tiled=True)
    total = jnp.zeros((slab_len, piece.shape[1]), jnp.float32)
    for tap in range(kernel):
        window = padded[2 * half - tap : 2 * half - tap + slab_len]
        total = total + lax.dot_general(
            window, piece[tap], (((1,), (1,)), ((), ())), preferred_element_type=jnp.float32
        )
    input_grad = total.astype(jnp.bfloat16)
    pair_sum = lax.psum(pair_part, ("dp", "seq"))
    scale = 1.0 / math.sqrt(lax.axis_size("dp") * seq_count * seq_count * slot_count)
    return (input_grad[None], pair_sum * scale)


def solution(mesh):
    in_specs = (
        P("dp", "seq", None),
        P("dp", None, "seq"),
        P(None, "dp", None),
        P(),
        P("dp", "seq", None, None),
        P("dp", "seq", None, None),
        P("dp", "seq", None, None),
        P("dp", None, None),
    )
    out_specs = (P("dp", "seq", None), P())
    return jax.shard_map(
        per_device, mesh=mesh, in_specs=in_specs, out_specs=out_specs, check_vma=False
    )
```

profile of v0, /device:TPU:0, one launch (start us, length us, event | category | flops | bytes accessed | tf_op | source)
XLA Modules:
  0.0 200.0 jit_solution(1862598864620470224)
XLA Ops:
  8.0 0.0 copy-start
  8.0 1.3 fusion.6
  9.3 0.0 copy-start.4
  9.3 0.7 compare_select_fusion
  10.0 1.9 gather_fusion
  11.9 4.3 %all-to-all-start.1 = ((bf16[2,128,768]{2,1,0:T(8,128)(2,1)}), bf16[2,128,768]{2,1,0:T(8,128)(2,1)S(1)}, u32[]{:S(2)}, u32[]{:S(2)}) async-start(bf16[2,128,768]{2,1,0:T(8,128)(2,1)} %bitcast.9), calls=%async_computation.1 | async-start | bytes 786432 | tf_op jit(solution)/shard_map/all_to_all | solution.py:50
  16.3 0.0 all-reduce.2.cloned.1.call-start
  16.3 0.0 copy-done.4
  16.3 1.2 gather_fusion.1
  17.5 0.0 copy-done.5
  17.5 0.2 dynamic-slice_reduce_fusion
  17.7 0.0 copy-done.6
  17.7 0.1 bitcast_select_fusion
  17.8 5.8 %all-to-all-done.1 = bf16[2,128,768]{2,1,0:T(8,128)(2,1)S(1)} async-done(((bf16[2,128,768]{2,1,0:T(8,128)(2,1)}), bf16[2,128,768]{2,1,0:T(8,128)(2,1)S(1)}, u32[]{:S(2)}, u32[]{:S(2)}) %all-to-all-start.1) | async-done | bytes 393248 | tf_op jit(solution)/shard_map/all_to_all | solution.py:50
  23.6 2.0 fusion.26
  25.6 0.0 all-reduce.2.cloned.1.call-update
  25.6 0.0 all-gather.2.cloned.1.call-start
  25.6 0.5 all-gather.2.cloned.1.call-update
  26.2 0.3 copy.19
  26.5 0.5 broadcast.65
  27.0 1.8 reduce.2
  28.8 0.7 reshape.152
  29.5 3.4 %all-to-all-start = ((bf16[2,2,24576]{2,1,0:T(2,128)(2,1)}), bf16[2,2,24576]{2,1,0:T(2,128)(2,1)S(1)}, u32[]{:S(2)}, u32[]{:S(2)}) async-start(bf16[2,2,24576]{2,1,0:T(2,128)(2,1)} %reshape.152), calls=%async_computation | async-start | bytes 393216 | tf_op jit(solution)/shard_map/all_to_all | solution.py:46
  33.0 1.3 convolution_convert_fusion
  34.3 4.3 %all-to-all-done = bf16[2,2,24576]{2,1,0:T(2,128)(2,1)S(1)} async-done(((bf16[2,2,24576]{2,1,0:T(2,128)(2,1)}), bf16[2,2,24576]{2,1,0:T(2,128)(2,1)S(1)}, u32[]{:S(2)}, u32[]{:S(2)}) %all-to-all-start) | async-done | bytes 196640 | tf_op jit(solution)/shard_map/all_to_all | solution.py:46
  38.6 4.2 %all-to-all-start.2 = ((bf16[2,128,768]{2,1,0:T(8,128)(2,1)}), bf16[2,128,768]{2,1,0:T(8,128)(2,1)}, u32[]{:S(2)}, u32[]{:S(2)}) async-start(bf16[2,128,768]{2,1,0:T(8,128)(2,1)} %bitcast.13), calls=%async_computation.2 | async-start | bytes 786432 | tf_op jit(solution)/shard_map/all_to_all | solution.py:67
  42.8 0.2 reshape.153
  43.0 0.2 copy.15
  43.2 0.2 copy.16
  43.4 0.3 broadcast_in_dim.10
  43.7 0.5 reshape.111
  44.2 0.5 convolution_multiply_fusion
  44.7 0.0 copy-start.1
  44.7 2.5 %scatter_fusion = f32[256,768]{1,0:T(8,128)S(1)} fusion(f32[256,768]{1,0:T(8,128)S(1)} %reshape.111, s32[256]{0:T(256)S(1)} %bitcast.77, f32[256,768]{1,0:T(8,128)S(1)} %convolution_multiply_fusion), kind=kCustom, calls=%fused_computation.2 | custom fusion | flops 196608 | bytes 2360320 | tf_op jit(solution)/shard_map/scatter-add | solution.py:76
  47.3 2.6 %all-to-all-done.2 = bf16[2,128,768]{2,1,0:T(8,128)(2,1)} async-done(((bf16[2,128,768]{2,1,0:T(8,128)(2,1)}), bf16[2,128,768]{2,1,0:T(8,128)(2,1)}, u32[]{:S(2)}, u32[]{:S(2)}) %all-to-all-start.2) | async-done | bytes 393248 | tf_op jit(solution)/shard_map/all_to_all | solution.py:67
  49.9 3.0 %scatter_custom_fusion.1 = f32[256,768]{1,0:T(8,128)S(1)} fusion(f32[256,768]{1,0:T(8,128)S(1)} %scatter_fusion, s32[256]{0:T(256)S(1)} %bitcast.79, bf16[256,768]{1,0:T(8,128)(2,1)} %bitcast.27), kind=kCustom, calls=%fused_computation.33 | custom fusion | flops 393216 | bytes 1179648 | tf_op jit(solution)/shard_map/scatter-add | solution.py:78
  52.9 0.4 fusion.11
  53.3 1.3 collective-permute-start
  54.6 4.7 %collective-permute-start.1 = (bf16[1,2,768]{2,1,0:T(2,128)(2,1)S(1)}, bf16[1,2,768]{2,1,0:T(2,128)(2,1)S(1)}, u32[]{:S(2)}, u32[]{:S(2)}) collective-permute-start(bf16[1,2,768]{2,1,0:T(2,128)(2,1)S(1)} %get-tuple-element.2), channel_id=1, source_target_pairs={{0,1},{2,3},{4,5},{6,7},{8,9},{10,11},{12,13},{14,15},{16,17},{18,... | collective-permute-start | bytes 9224 | tf_op jit(solution)/shard_map/ppermute | solution.py:15
  59.3 123.8 %all-reduce.2.cloned.1.call-done = f32[768,768]{1,0:T(8,128)} async-done(((f32[768,768]{1,0:T(8,128)}), f32[768,768]{1,0:T(8,128)}) %all-reduce.2.cloned.1.call-update) | async-done | bytes 2359312 | tf_op jit(solution)/shard_map/psum | solution.py:90
  183.1 3.3 %broadcast_multiply_fusion = f32[768,768]{1,0:T(8,128)} fusion(f32[768,768]{1,0:T(8,128)} %all-reduce.2.cloned.1.call-done), kind=kLoop, calls=%fused_computation.23 | loop fusion | flops 589824 | bytes 4718592 | tf_op jit(solution)/shard_map/mul | solution.py:92
  186.4 0.0 collective-permute-done
  186.4 1.9 fusion.2
  188.3 1.9 convolution_add_fusion.3
  190.3 0.5 convolution_add_fusion.2
  190.8 0.0 collective-permute-done.1
  190.8 0.5 convolution_add_fusion.1
  191.3 1.3 fusion.1
  (14 shorter events, 0.1 us)
Async XLA Ops:
  8.0 25.0 %copy-start = (bf16[768,768]{1,0:T(8,128)(2,1)S(1)}, bf16[768,768]{1,0:T(8,128)(2,1)}, u32[]{:S(2)}) copy-start(bf16[768,768]{1,0:T(8,128)(2,1)} %param.11) | copy-start | bytes 3538948
  9.3 7.0 %copy-start.4 = (s32[1,1,2,128]{3,2,1,0:T(2,128)S(1)}, s32[1,1,2,128]{3,2,1,0:T(2,128)}, u32[]{:S(2)}) copy-start(s32[1,1,2,128]{3,2,1,0:T(2,128)} %param.13) | copy-start | bytes 3076
  11.9 5.6 %copy-start.5 = (s32[1,2,2]{2,1,0:T(2,128)S(1)}, s32[1,2,2]{2,1,0:T(2,128)}, u32[]{:S(2)}) copy-start(s32[1,2,2]{2,1,0:T(2,128)} %param.15) | copy-start | bytes 52
  11.9 5.8 %copy-start.6 = (f32[1,1,2,128]{3,2,1,0:T(2,128)S(1)}, f32[1,1,2,128]{3,2,1,0:T(2,128)}, u32[]{:S(2)}) copy-start(f32[1,1,2,128]{3,2,1,0:T(2,128)} %param.14) | copy-start | bytes 3076
  11.9 11.6 %all-to-all-start.1 = ((bf16[2,128,768]{2,1,0:T(8,128)(2,1)}), bf16[2,128,768]{2,1,0:T(8,128)(2,1)S(1)}, u32[]{:S(2)}, u32[]{:S(2)}) async-start(bf16[2,128,768]{2,1,0:T(8,128)(2,1)} %bitcast.9), calls=%async_computation.1 | async-start | bytes 786432 | tf_op jit(solution)/shard_map/all_to_all | solution.py:50
  16.3 166.8 %all-reduce.2.cloned.1.call-start = ((), (), s32[]{:S(2)}) async-start(), calls=%async_computation.4 | async-start | bytes 4718592 | tf_op jit(solution)/shard_map/psum | solution.py:90
  23.6 2.6 %copy-start.3 = (bf16[1,256,384]{2,1,0:T(8,128)(2,1)S(1)}, bf16[1,256,384]{2,1,0:T(8,128)(2,1)}, u32[]{:S(2)}) copy-start(bf16[1,256,384]{2,1,0:T(8,128)(2,1)} %param.9) | copy-start | bytes 589828
  25.6 160.8 %all-gather.2.cloned.1.call-start = ((), (), s32[]{:S(2)}) async-start(), calls=%async_computation.3 | async-start | bytes 6266880 | tf_op jit(solution)/shard_map/all_gather | solution.py:82
  29.5 9.0 %all-to-all-start = ((bf16[2,2,24576]{2,1,0:T(2,128)(2,1)}), bf16[2,2,24576]{2,1,0:T(2,128)(2,1)S(1)}, u32[]{:S(2)}, u32[]{:S(2)}) async-start(bf16[2,2,24576]{2,1,0:T(2,128)(2,1)} %reshape.152), calls=%async_computation | async-start | bytes 393216 | tf_op jit(solution)/shard_map/all_to_all | solution.py:46
  38.6 11.3 %all-to-all-start.2 = ((bf16[2,128,768]{2,1,0:T(8,128)(2,1)}), bf16[2,128,768]{2,1,0:T(8,128)(2,1)}, u32[]{:S(2)}, u32[]{:S(2)}) async-start(bf16[2,128,768]{2,1,0:T(8,128)(2,1)} %bitcast.13), calls=%async_computation.2 | async-start | bytes 786432 | tf_op jit(solution)/shard_map/all_to_all | solution.py:67
  44.7 8.2 %copy-start.1 = (bf16[1,256,768]{2,1,0:T(8,128)(2,1)S(1)}, bf16[1,256,768]{2,1,0:T(8,128)(2,1)}, u32[]{:S(2)}) copy-start(bf16[1,256,768]{2,1,0:T(8,128)(2,1)} %param.8) | copy-start | bytes 1179652
  53.3 133.1 %collective-permute-start = (bf16[1,2,768]{2,1,0:T(2,128)(2,1)S(1)}, bf16[1,2,768]{2,1,0:T(2,128)(2,1)S(1)}, u32[]{:S(2)}, u32[]{:S(2)}) collective-permute-start(bf16[1,2,768]{2,1,0:T(2,128)(2,1)S(1)} %get-tuple-element.3), channel_id=1, source_target_pairs={{1,0},{3,2},{5,4},{7,6},{9,8},{11,10},{13,12},{15,14},{17,16},{19,... | collective-permute-start | bytes 9224 | tf_op jit(solution)/shard_map/ppermute | solution.py:16
  54.6 136.2 %collective-permute-start.1 = (bf16[1,2,768]{2,1,0:T(2,128)(2,1)S(1)}, bf16[1,2,768]{2,1,0:T(2,128)(2,1)S(1)}, u32[]{:S(2)}, u32[]{:S(2)}) collective-permute-start(bf16[1,2,768]{2,1,0:T(2,128)(2,1)S(1)} %get-tuple-element.2), channel_id=1, source_target_pairs={{0,1},{2,3},{4,5},{6,7},{8,9},{10,11},{12,13},{14,15},{16,17},{18,... | collective-permute-start | bytes 9224 | tf_op jit(solution)/shard_map/ppermute | solution.py:15
  186.4 3.9 %copy-start.2 = (bf16[5,768,768]{2,1,0:T(8,128)(2,1)S(1)}, bf16[5,768,768]{2,1,0:T(8,128)(2,1)}, u32[]{:S(2)}) copy-start(bf16[5,768,768]{2,1,0:T(8,128)(2,1)} %all-gather.2.cloned.1.call-done) | copy-start | bytes 17694724
Sparse Core Ops, SparseCore 0:
  25.7 157.3 all-reduce.1
Sparse Core Ops, SparseCore 1:
  28.3 64.0 all-gather.1
where the time goes:
time: 200 us
  waiting for transfers between devices  137 us (68%)
  starting transfers between devices  18 us (9%)
  between operations  15.7 us (8%)
  other arithmetic  13.1 us (7%)
  matrix products  9.85 us (5%)
  local copies, waits for them, and re-layouts  6.27 us (3%)
    psum x1, waiting for transfers between devices, per_device(): pair_sum = lax.psum(pair_part, ('dp', 'seq'))  124 us
    dot_general x5, matrix products, per_device(): lax.dot_general(window, piece[tap], (((1,), (1,)), ((), ())), preferred_e...  6.13 us
    all_to_all x1, waiting for transfers between devices, per_device(): lax.all_to_all(outgoing, 'seq', split_axis=0, concat_axis=0, tiled=True)  5.81 us
    scatter-add x2, other arithmetic, per_device(): act_grad = pooled.at[accept_index].add(accept_term).at[send_index].add(re...  5.57 us
    ppermute x1, starting transfers between devices, with_halo(): before = lax.ppermute(last, axis, up)  4.72 us
    all_to_all x1, starting transfers between devices, per_device(): lax.all_to_all(outgoing, 'seq', split_axis=0, concat_axis=0, tiled=True)  4.34 us
    all_to_all x1, waiting for transfers between devices, per_device(): lax.all_to_all(trunk_grad, 'seq', split_axis=1, concat_axis=2, tiled=True)  4.32 us
    all_to_all x1, starting transfers between devices, per_device(): lax.all_to_all(donor_term.reshape(seq_count, slot_count, channels), 'seq'...  4.17 us
  transfers between devices with their start and end apart: 7, of which 4 were waited for; matrix products, arithmetic and copies ran while one was open for 11% of the time, Pallas kernels for 0%

commit v1 on v0

--- a/solution.py
+++ b/solution.py
@@ -3,6 +3,7 @@
 import jax.numpy as jnp
 from jax import lax
 from jax.sharding import PartitionSpec as P
+from jax.lax import all_to_all, axis_size
 
 
 def with_halo(x, sides, width):
@@ -43,7 +44,10 @@
     half = kernel // 2
     act_f, slope = gelu_parts(pre_act[0].astype(jnp.float32))
     act = act_f.astype(jnp.bfloat16)
-    arrived = lax.all_to_all(trunk_grad, "seq", split_axis=1, concat_axis=2, tiled=True)
+    arrived = jnp.concatenate(
+        all_to_all(jnp.stack(jnp.split(trunk_grad, axis_size("seq"), axis=1), axis=0), "seq", 0, 0),
+        axis=2,
+    )
     pooled = jnp.repeat(arrived[0].astype(jnp.float32) * 0.5, 2, axis=0)
     send_index = donor_slots[0, 0].reshape(-1)
     outgoing = act[send_index].reshape(seq_count, slot_count, channels)

time: 200 us -> 200 us (level)
  waiting for transfers between devices: 137 us -> 140 us
    psum x1, waiting for transfers between devices: 124 us -> 127 us  [per_device(): pair_sum = lax.psum(pair_part, ('dp', 'seq'))]
  transfers between devices with their start and end apart: 7 -> 7, of which waited for: 4 -> 4; matrix products, arithmetic and copies ran while one was open for 11% -> 9% of each run, Pallas kernels for 0% -> 0%
where the time goes in v1:
time: 200 us
  waiting for transfers between devices  140 us (70%)
  starting transfers between devices  17.8 us (9%)
  between operations  15.7 us (8%)
  other arithmetic  12 us (6%)
  matrix products  9.85 us (5%)
  local copies, waits for them, and re-layouts  4.6 us (2%)
    psum x1, waiting for transfers between devices, per_device(): pair_sum = lax.psum(pair_part, ('dp', 'seq'))  127 us
    dot_general x5, matrix products, per_device(): lax.dot_general(window, piece[tap], (((1,), (1,)), ((), ())), preferred_e...  6.13 us
    all_to_all x1, waiting for transfers between devices, per_device(): lax.all_to_all(outgoing, 'seq', split_axis=0, concat_axis=0, tiled=True)  5.81 us
    scatter-add x2, other arithmetic, per_device(): act_grad = pooled.at[accept_index].add(accept_term).at[send_index].add(re...  5.58 us
    ppermute x1, starting transfers between devices, with_halo(): before = lax.ppermute(last, axis, up)  4.54 us
    all_to_all x1, waiting for transfers between devices, per_device(): all_to_all(jnp.stack(jnp.split(trunk_grad, axis_size('seq'), axis=1), axi...  4.52 us
    all_to_all x1, starting transfers between devices, per_device(): lax.all_to_all(outgoing, 'seq', split_axis=0, concat_axis=0, tiled=True)  4.34 us
    all_to_all x1, starting transfers between devices, per_device(): lax.all_to_all(donor_term.reshape(seq_count, slot_count, channels), 'seq'...  4.15 us
  transfers between devices with their start and end apart: 7, of which 4 were waited for; matrix products, arithmetic and copies ran while one was open for 9% of the time, Pallas kernels for 0%

profile of v1, /device:TPU:0, one launch (start us, length us, event | category | flops | bytes accessed | tf_op | source)
XLA Modules:
  0.0 199.7 jit_solution(14936559200213618644)
XLA Ops:
  8.0 0.0 copy-start
  8.0 1.3 fusion.6
  9.3 0.0 copy-start.4
  9.3 0.7 compare_select_fusion
  10.0 1.9 gather_fusion
  11.9 4.3 %all-to-all-start.1 = ((bf16[2,128,768]{2,1,0:T(8,128)(2,1)}), bf16[2,128,768]{2,1,0:T(8,128)(2,1)S(1)}, u32[]{:S(2)}, u32[]{:S(2)}) async-start(bf16[2,128,768]{2,1,0:T(8,128)(2,1)} %bitcast.11), calls=%async_computation.1 | async-start | bytes 786432 | tf_op jit(solution)/shard_map/all_to_all | solution.py:54
  16.3 0.0 all-reduce.2.cloned.1.call-start
  16.3 0.0 copy-done.4
  16.3 1.2 gather_fusion.1
  17.5 0.0 copy-done.5
  17.5 0.2 dynamic-slice_reduce_fusion
  17.7 0.0 copy-done.6
  17.7 0.1 bitcast_select_fusion
  17.8 5.8 %all-to-all-done.1 = bf16[2,128,768]{2,1,0:T(8,128)(2,1)S(1)} async-done(((bf16[2,128,768]{2,1,0:T(8,128)(2,1)}), bf16[2,128,768]{2,1,0:T(8,128)(2,1)S(1)}, u32[]{:S(2)}, u32[]{:S(2)}) %all-to-all-start.1) | async-done | bytes 393248 | tf_op jit(solution)/shard_map/all_to_all | solution.py:54
  23.6 2.0 fusion.26
  25.6 0.0 all-reduce.2.cloned.1.call-update
  25.6 0.0 all-gather.2.cloned.1.call-start
  25.6 0.5 all-gather.2.cloned.1.call-update
  26.2 0.0 copy-done.3
  26.2 0.1 copy.17
  26.3 0.1 copy.18
  26.5 0.7 pad_maximum_fusion.2
  27.1 3.4 %all-to-all-start = ((bf16[2,1,128,384]{2,3,1,0:T(8,128)(2,1)}), bf16[2,1,128,384]{2,3,1,0:T(8,128)(2,1)S(1)}, u32[]{:S(2)}, u32[]{:S(2)}) async-start(bf16[2,1,128,384]{2,3,1,0:T(8,128)(2,1)} %pad_maximum_fusion.2), calls=%async_computation | async-start | bytes 393216 | tf_op jit(solution)/shard_map/all_to_all | solution.py:48
  30.6 1.3 convolution_convert_fusion
  31.9 4.5 %all-to-all-done = bf16[2,1,128,384]{2,3,1,0:T(8,128)(2,1)S(1)} async-done(((bf16[2,1,128,384]{2,3,1,0:T(8,128)(2,1)}), bf16[2,1,128,384]{2,3,1,0:T(8,128)(2,1)S(1)}, u32[]{:S(2)}, u32[]{:S(2)}) %all-to-all-start) | async-done | bytes 196640 | tf_op jit(solution)/shard_map/all_to_all | solution.py:48
  36.4 4.2 %all-to-all-start.2 = ((bf16[2,128,768]{2,1,0:T(8,128)(2,1)}), bf16[2,128,768]{2,1,0:T(8,128)(2,1)}, u32[]{:S(2)}, u32[]{:S(2)}) async-start(bf16[2,128,768]{2,1,0:T(8,128)(2,1)} %bitcast.15), calls=%async_computation.2 | async-start | bytes 786432 | tf_op jit(solution)/shard_map/all_to_all | solution.py:71
  40.6 0.2 copy.16
  40.8 0.3 broadcast_in_dim.10
  41.0 0.5 reshape.108
  41.6 0.5 convolution_multiply_fusion
  42.1 0.0 copy-start.1
  42.1 2.5 %scatter_fusion = f32[256,768]{1,0:T(8,128)S(1)} fusion(f32[256,768]{1,0:T(8,128)S(1)} %reshape.108, s32[256]{0:T(256)S(1)} %bitcast.75, f32[256,768]{1,0:T(8,128)S(1)} %convolution_multiply_fusion), kind=kCustom, calls=%fused_computation.2 | custom fusion | flops 196608 | bytes 2360320 | tf_op jit(solution)/shard_map/scatter-add | solution.py:80
  44.6 1.9 all-to-all-done.2
  46.5 3.0 %scatter_custom_fusion.1 = f32[256,768]{1,0:T(8,128)S(1)} fusion(f32[256,768]{1,0:T(8,128)S(1)} %scatter_fusion, s32[256]{0:T(256)S(1)} %bitcast.77, bf16[256,768]{1,0:T(8,128)(2,1)} %bitcast.29), kind=kCustom, calls=%fused_computation.33 | custom fusion | flops 393216 | bytes 1179648 | tf_op jit(solution)/shard_map/scatter-add | solution.py:82
  49.6 0.0 copy-done.1
  49.6 0.4 fusion.11
  49.9 1.3 collective-permute-start
  51.2 4.5 %collective-permute-start.1 = (bf16[1,2,768]{2,1,0:T(2,128)(2,1)S(1)}, bf16[1,2,768]{2,1,0:T(2,128)(2,1)S(1)}, u32[]{:S(2)}, u32[]{:S(2)}) collective-permute-start(bf16[1,2,768]{2,1,0:T(2,128)(2,1)S(1)} %get-tuple-element.2), channel_id=1, source_target_pairs={{0,1},{2,3},{4,5},{6,7},{8,9},{10,11},{12,13},{14,15},{16,17},{18,... | collective-permute-start | bytes 9224 | tf_op jit(solution)/shard_map/ppermute | solution.py:16
  55.8 127.0 %all-reduce.2.cloned.1.call-done = f32[768,768]{1,0:T(8,128)} async-done(((f32[768,768]{1,0:T(8,128)}), f32[768,768]{1,0:T(8,128)}) %all-reduce.2.cloned.1.call-update) | async-done | bytes 2359312 | tf_op jit(solution)/shard_map/psum | solution.py:94
  182.8 3.3 %broadcast_multiply_fusion = f32[768,768]{1,0:T(8,128)} fusion(f32[768,768]{1,0:T(8,128)} %all-reduce.2.cloned.1.call-done), kind=kLoop, calls=%fused_computation.23 | loop fusion | flops 589824 | bytes 4718592 | tf_op jit(solution)/shard_map/mul | solution.py:96
  186.1 0.0 collective-permute-done
  186.1 1.9 fusion.2
  188.0 1.9 convolution_add_fusion.3
  190.0 0.0 copy-done.2
  190.0 0.5 convolution_add_fusion.2
  190.5 0.0 collective-permute-done.1
  190.5 0.5 convolution_add_fusion.1
  191.0 1.3 fusion.1
  (12 shorter events, 0.1 us)
Async XLA Ops:
  8.0 22.6 %copy-start = (bf16[768,768]{1,0:T(8,128)(2,1)S(1)}, bf16[768,768]{1,0:T(8,128)(2,1)}, u32[]{:S(2)}) copy-start(bf16[768,768]{1,0:T(8,128)(2,1)} %param.11) | copy-start | bytes 3538948
  9.3 7.0 %copy-start.4 = (s32[1,1,2,128]{3,2,1,0:T(2,128)S(1)}, s32[1,1,2,128]{3,2,1,0:T(2,128)}, u32[]{:S(2)}) copy-start(s32[1,1,2,128]{3,2,1,0:T(2,128)} %param.13) | copy-start | bytes 3076
  11.9 5.6 %copy-start.5 = (s32[1,2,2]{2,1,0:T(2,128)S(1)}, s32[1,2,2]{2,1,0:T(2,128)}, u32[]{:S(2)}) copy-start(s32[1,2,2]{2,1,0:T(2,128)} %param.15) | copy-start | bytes 52
  11.9 5.8 %copy-start.6 = (f32[1,1,2,128]{3,2,1,0:T(2,128)S(1)}, f32[1,1,2,128]{3,2,1,0:T(2,128)}, u32[]{:S(2)}) copy-start(f32[1,1,2,128]{3,2,1,0:T(2,128)} %param.14) | copy-start | bytes 3076
  11.9 11.6 %all-to-all-start.1 = ((bf16[2,128,768]{2,1,0:T(8,128)(2,1)}), bf16[2,128,768]{2,1,0:T(8,128)(2,1)S(1)}, u32[]{:S(2)}, u32[]{:S(2)}) async-start(bf16[2,128,768]{2,1,0:T(8,128)(2,1)} %bitcast.11), calls=%async_computation.1 | async-start | bytes 786432 | tf_op jit(solution)/shard_map/all_to_all | solution.py:54
  16.3 166.6 %all-reduce.2.cloned.1.call-start = ((), (), s32[]{:S(2)}) async-start(), calls=%async_computation.4 | async-start | bytes 4718592 | tf_op jit(solution)/shard_map/psum | solution.py:94
  23.6 2.6 %copy-start.3 = (bf16[1,256,384]{2,1,0:T(8,128)(2,1)S(1)}, bf16[1,256,384]{2,1,0:T(8,128)(2,1)}, u32[]{:S(2)}) copy-start(bf16[1,256,384]{2,1,0:T(8,128)(2,1)} %param.9) | copy-start | bytes 589828
  25.6 160.5 %all-gather.2.cloned.1.call-start = ((), (), s32[]{:S(2)}) async-start(), calls=%async_computation.3 | async-start | bytes 6266880 | tf_op jit(solution)/shard_map/all_gather | solution.py:86
  27.1 9.2 %all-to-all-start = ((bf16[2,1,128,384]{2,3,1,0:T(8,128)(2,1)}), bf16[2,1,128,384]{2,3,1,0:T(8,128)(2,1)S(1)}, u32[]{:S(2)}, u32[]{:S(2)}) async-start(bf16[2,1,128,384]{2,3,1,0:T(8,128)(2,1)} %pad_maximum_fusion.2), calls=%async_computation | async-start | bytes 393216 | tf_op jit(solution)/shard_map/all_to_all | solution.py:48
  36.4 10.1 %all-to-all-start.2 = ((bf16[2,128,768]{2,1,0:T(8,128)(2,1)}), bf16[2,128,768]{2,1,0:T(8,128)(2,1)}, u32[]{:S(2)}, u32[]{:S(2)}) async-start(bf16[2,128,768]{2,1,0:T(8,128)(2,1)} %bitcast.15), calls=%async_computation.2 | async-start | bytes 786432 | tf_op jit(solution)/shard_map/all_to_all | solution.py:71
  42.1 7.5 %copy-start.1 = (bf16[1,256,768]{2,1,0:T(8,128)(2,1)S(1)}, bf16[1,256,768]{2,1,0:T(8,128)(2,1)}, u32[]{:S(2)}) copy-start(bf16[1,256,768]{2,1,0:T(8,128)(2,1)} %param.8) | copy-start | bytes 1179652
  49.9 136.2 %collective-permute-start = (bf16[1,2,768]{2,1,0:T(2,128)(2,1)S(1)}, bf16[1,2,768]{2,1,0:T(2,128)(2,1)S(1)}, u32[]{:S(2)}, u32[]{:S(2)}) collective-permute-start(bf16[1,2,768]{2,1,0:T(2,128)(2,1)S(1)} %get-tuple-element.3), channel_id=1, source_target_pairs={{1,0},{3,2},{5,4},{7,6},{9,8},{11,10},{13,12},{15,14},{17,16},{19,... | collective-permute-start | bytes 9224 | tf_op jit(solution)/shard_map/ppermute | solution.py:17
  51.2 139.2 %collective-permute-start.1 = (bf16[1,2,768]{2,1,0:T(2,128)(2,1)S(1)}, bf16[1,2,768]{2,1,0:T(2,128)(2,1)S(1)}, u32[]{:S(2)}, u32[]{:S(2)}) collective-permute-start(bf16[1,2,768]{2,1,0:T(2,128)(2,1)S(1)} %get-tuple-element.2), channel_id=1, source_target_pairs={{0,1},{2,3},{4,5},{6,7},{8,9},{10,11},{12,13},{14,15},{16,17},{18,... | collective-permute-start | bytes 9224 | tf_op jit(solution)/shard_map/ppermute | solution.py:16
  186.1 3.9 %copy-start.2 = (bf16[5,768,768]{2,1,0:T(8,128)(2,1)S(1)}, bf16[5,768,768]{2,1,0:T(8,128)(2,1)}, u32[]{:S(2)}) copy-start(bf16[5,768,768]{2,1,0:T(8,128)(2,1)} %all-gather.2.cloned.1.call-done) | copy-start | bytes 17694724
Sparse Core Ops, SparseCore 0:
  25.7 157.0 all-reduce.1
Sparse Core Ops, SparseCore 1:
  28.3 63.6 all-gather.1
